TPU v7x, 32 devices: a whole 2x2x4 slice. The times are simulated.
32 devices in a mesh: dp: 4 (over z), ctx: 8 (over y, x, core).
Axes of the slice: x: 2, y: 2, z: 4, core: 2. Of those that a mesh axis runs over, the one named last changes fastest.
Arguments:
- tokens: float32 [16, 2048, 768], P('dp', 'ctx'), may hold values from -6 to 6
- cotangent: float32 [16, 2048, 768], P('dp', 'ctx'), may hold values from -6 to 6
- lengths: int32 [16], replicated, may hold values from 1024 to 2048, as said below
- w_query: bfloat16 [768, 768], P(('dp', 'ctx')), may hold values from -0.21875 to 0.21875
- w_key: bfloat16 [768, 768], P(('dp', 'ctx')), may hold values from -0.21875 to 0.21875
- w_value: bfloat16 [768, 768], P(('dp', 'ctx')), may hold values from -0.21875 to 0.21875
- w_attn_out: bfloat16 [768, 768], P(('dp', 'ctx')), may hold values from -6 to 6
- w_up: bfloat16 [768, 3072], P(('dp', 'ctx')), may hold values from -0.21875 to 0.21875
- b_up: bfloat16 [3072], P(('dp', 'ctx')), may hold values from -4 to 4
- w_down: bfloat16 [3072, 768], P(('dp', 'ctx')), may hold values from -0.109375 to 0.109375
- vectors: bfloat16 [8, 768], P(None, ('dp', 'ctx')), may hold values from -0.6 to 1.4
Outputs:
- output: float32 [16, 2048, 768], P('dp', 'ctx')
- d_tokens: float32 [16, 2048, 768], P('dp', 'ctx')
- d_w_query: float32 [768, 768], P(('dp', 'ctx'))
- d_w_key: float32 [768, 768], P(('dp', 'ctx'))
- d_w_value: float32 [768, 768], P(('dp', 'ctx'))
- d_w_attn_out: float32 [768, 768], P(('dp', 'ctx'))
- d_w_up: float32 [768, 3072], P(('dp', 'ctx'))
- d_b_up: float32 [3072], P(('dp', 'ctx'))
- d_w_down: float32 [3072, 768], P(('dp', 'ctx'))
- d_vectors: float32 [8, 768], P(None, ('dp', 'ctx'))
Inputs may be any that keep to these rules, and one draw needn't show every extreme that they name: `lengths`: each sequence fills 2048 / 2 to 2048 of its 2048 slots; among the 4 sequences of every index of dp one has length 2048.
All inputs are finite; a program needn't handle non-finite values.
Results may differ from a plain program's by a relative error of at most 0.018.
The roundings to bfloat16 on the way count: a program that leaves them out, or rounds other values in their place, can miss the bound.
Values may be sent and summed in bfloat16 or wider, within the bound.
A program may use at most 320 MiB of HBM per device.

v0:
```python
import functools
import jax
import jax.numpy as jnp
from jax import lax
from jax.experimental import pallas as pl
from jax.experimental.pallas import tpu as pltpu
from jax.sharding import PartitionSpec as P

HEAD_DIM = 64
F32 = jnp.float32
BF = jnp.bfloat16
NN = (((1,), (0,)), ((), ()))
NT = (((1,), (1,)), ((), ()))
TN = (((0,), (0,)), ((), ()))
epsilon = 1e-12
masked_score = -1e30
VMEM_BYTES = 58 << 20


def dg(left, right, dims):
    return lax.dot_general(left, right, dims, preferred_element_type=F32)


MESH = pl.DeviceIdType.MESH


class Mover:
    def __init__(self, local_sem, send_sem, recv_sem):
        self.local_sem, self.send_sem, self.recv_sem = local_sem, send_sem, recv_sem
        self.locals = self.remotes = 0

    def local(self, source, target):
        copy = pltpu.make_async_copy(source, target, self.local_sem.at[self.locals])
        self.locals += 1
        return copy

    def remote(self, source, target, device):
        number = self.remotes
        self.remotes += 1
        return pltpu.make_async_remote_copy(
            src_ref=source,
            dst_ref=target,
            send_sem=self.send_sem.at[number],
            recv_sem=self.recv_sem.at[number],
            device_id=device,
            device_id_type=MESH,
        )


def greet(devices):
    barrier = pltpu.get_barrier_semaphore()
    for device in devices:
        pl.semaphore_signal(barrier, inc=1, device_id=device, device_id_type=MESH)
    pl.semaphore_wait(barrier, len(devices))


def place(dp, ctx):
    d, c = lax.axis_index("dp"), lax.axis_index("ctx")
    groups = ctx // 2
    g, m = c // 2, c % 2
    over_dp = [((d + k) % dp, c) for k in range(1, dp)]
    over_groups = [(d, (g + k) % groups * 2 + m) for k in range(1, groups)]
    return d, c, g, m, over_dp, over_groups, (d, g * 2 + 1 - m)


def flip(group, step, groups):
    total, bit = 0, 1
    while bit < groups:
        total = total + (group // bit + step // bit) % 2 * bit
        bit *= 2
    return total


def gather_kernel(dp, ctx, *refs):
    (tokens, cotangent, w, wo, wu, wd), refs = refs[:6], refs[6:]
    (x_in, rest_to, up_to, w_full, zo, zu, zd), refs = refs[:7], refs[7:]
    wide, wide_up, x, rest, up, local_sem, send_sem, recv_sem, move_sem = refs
    d, c, g, m, over_dp, over_groups, sibling = place(dp, ctx)
    groups = ctx // 2
    moves = [
        pltpu.make_async_copy(source, target, move_sem.at[i])
        for i, (source, target) in enumerate(
            ((tokens, wide), (cotangent, wide_up), (rest, rest_to), (up, up_to))
        )
    ]
    moves[0].start()
    greet(over_dp + [(d, (c + k) % ctx) for k in range(1, ctx)])
    mover = Mover(local_sem, send_sem, recv_sem)
    own = [
        mover.local(source, target)
        for source, target in (
            (w, w_full.at[d, c]),
            (x.at[c], x_in.at[c]),
            (wo, zo.at[d]),
            (wu, zu.at[d]),
            (wd, zd.at[d]),
        )
    ]
    along = [mover.remote(w, w_full.at[d, c], device) for device in over_dp]
    across = [[mover.remote(w, w_full.at[d, c], device) for device in over_groups]]
    rows = [
        mover.remote(x.at[(c + k) % ctx], x_in.at[c], (d, (c + k) % ctx)) for k in range(1, ctx)
    ]
    others = [
        mover.remote(source, target.at[d], device)
        for source, target in ((wo, zo), (wu, zu), (wd, zd))
        for device in over_dp
    ]
    for copy in along + across[0]:
        copy.start()
    moves[0].wait()
    moves[1].start()
    x[...] = wide[...].astype(BF)
    for copy in rows + own + others:
        copy.start()
    rest[...] = (wide[...] - x[...].astype(F32)).astype(BF)
    moves[2].start()
    moves[1].wait()
    up[...] = wide_up[...].astype(BF)
    moves[3].start()
    for k in range(1, dp):
        along[k - 1].wait_recv()
        piece = w_full.at[(d - k + dp) % dp, c]
        across.append([mover.remote(piece, piece, device) for device in over_groups])
        for copy in across[-1]:
            copy.start()
    own[0].wait()
    mine = w_full.at[:, c]
    over = [mover.remote(mine, mine, sibling)]
    over[0].start()
    for k in range(1, groups):
        for batch in across:
            batch[k - 1].wait_recv()
        block = w_full.at[:, (g - k + groups) % groups * 2 + m]
        over.append(mover.remote(block, block, sibling))
        over[-1].start()
    for copy in over + rows + others + moves[2:]:
        copy.wait()
    for copy in along + [copy for batch in across for copy in batch]:
        copy.wait_send()
    for copy in own[1:]:
        copy.wait()


def gather_first(tokens, cotangent, w, wo, wu, wd, dp, ctx):
    groups = ctx // 2
    remotes = (dp - 1) + dp * (groups - 1) + (ctx - 1) + 3 * (dp - 1) + groups
    any_space = pl.BlockSpec(memory_space=pl.ANY)
    return pl.pallas_call(
        functools.partial(gather_kernel, dp, ctx),
        in_specs=[any_space] * 6,
        out_specs=[any_space] * 7,
        out_shape=[jax.ShapeDtypeStruct(tokens.shape, BF)] * 3
        + [jax.ShapeDtypeStruct((dp, ctx) + w.shape, BF)]
        + [jax.ShapeDtypeStruct((dp,) + array.shape, BF) for array in (wo, wu, wd)],
        scratch_shapes=[pltpu.VMEM(tokens.shape, F32)] * 2
        + [pltpu.VMEM(tokens.shape, BF)] * 3
        + [
            pltpu.SemaphoreType.DMA((5,)),
            pltpu.SemaphoreType.DMA((remotes,)),
            pltpu.SemaphoreType.DMA((remotes,)),
            pltpu.SemaphoreType.DMA((4,)),
        ],
        compiler_params=pltpu.CompilerParams(
            collective_id=0, has_side_effects=True, vmem_limit_bytes=VMEM_BYTES
        ),
        name="gather_first",
    )(tokens, cotangent, w, wo, wu, wd)


class Spread:
    def __init__(self, dp, ctx, sources, targets, mover):
        d, c, g, m, over_dp, over_groups, sibling = place(dp, ctx)
        groups = ctx // 2
        self.devices = over_groups + [sibling]
        self.own = [mover.local(s, t.at[:, c]) for s, t in zip(sources, targets)]
        self.direct = [mover.remote(s, t.at[:, c], sibling) for s, t in zip(sources, targets)]
        self.across = [
            [mover.remote(s, t.at[:, c], device) for device in over_groups]
            for s, t in zip(sources, targets)
        ]
        self.onward = []
        for t in targets:
            blocks = [t.at[:, (g - k + groups) % groups * 2 + m] for k in range(1, groups)]
            self.onward.append([mover.remote(block, block, sibling) for block in blocks])

    @staticmethod
    def count(groups, arrays):
        return arrays * (1 + 2 * (groups - 1))

    def begin(self):
        greet(self.devices)
        for copy in self.own + [copy for batch in self.across for copy in batch] + self.direct:
            copy.start()

    def forward(self, index):
        for came, copy in zip(self.across[index], self.onward[index]):
            came.wait_recv()
            copy.start()

    def finish(self):
        for copy in self.own + self.direct + [copy for batch in self.onward for copy in batch]:
            copy.wait()
        for batch in self.across:
            for copy in batch:
                copy.wait_send()


class Scatter:
    def __init__(self, dp, ctx, sources, outs, buffers, small, small_out, small_buffers, mover):
        d, c, g, m, over_dp, over_groups, sibling = place(dp, ctx)
        groups = ctx // 2
        self.dp, self.groups, self.d, self.g = dp, groups, d, g
        self.devices = over_groups + over_dp + [sibling]
        self.outs = list(outs)
        self.buffers = buffers
        self.own, self.pair, self.across, self.along = [], [], [], []
        for source, (mine, other, came, sums, last) in zip(sources, buffers):
            summed = len(source.shape) == 4
            if summed:
                self.own.append(mover.local(source, mine))
                self.pair.append([])
            else:
                self.own.append(mover.local(source.at[:, :, m], mine))
                self.pair.append([mover.remote(source.at[:, :, 1 - m], other, sibling)])
            onward = source if summed else mine
            self.across.append(
                [
                    mover.remote(onward.at[:, (g + k) % groups], came.at[k - 1], over_groups[k - 1])
                    for k in range(1, groups)
                ]
            )
            self.along.append(
                [
                    mover.remote(sums.at[(d + k) % dp], last.at[k - 1], over_dp[k - 1])
                    for k in range(1, dp)
                ]
            )
        self.small, self.small_out = small, small_out
        one, came, two, groups_in, three, dp_in = small_buffers
        self.small_buffers = small_buffers
        self.pair.append([mover.remote(one, came, sibling)])
        self.across.append(
            [mover.remote(two, groups_in.at[k - 1], over_groups[k - 1]) for k in range(1, groups)]
        )
        self.along.append(
            [mover.remote(three, dp_in.at[k - 1], over_dp[k - 1]) for k in range(1, dp)]
        )

    @staticmethod
    def count(dp, ctx, arrays):
        return (arrays + 1) * (1 + ctx // 2 - 1 + dp - 1)

    @staticmethod
    def scratch(dp, ctx, sources, small):
        groups = ctx // 2
        shapes = []
        for s in sources:
            block = s.shape[-2:]
            shapes += [
                pltpu.VMEM((dp, groups) + block, BF),
                pltpu.VMEM((dp, groups) + block if len(s.shape) == 5 else (8, 128), BF),
                pltpu.VMEM((groups - 1, dp) + block, BF),
                pltpu.VMEM((dp,) + block, BF),
                pltpu.VMEM((dp - 1,) + block, BF),
            ]
        shape = small.shape
        shapes += [pltpu.VMEM(shape, F32)] * 3
        shapes += [
            pltpu.VMEM((groups - 1,) + shape, F32),
            pltpu.VMEM(shape, F32),
            pltpu.VMEM((dp - 1,) + shape, F32),
        ]
        return shapes

    def begin_small(self):
        self.small_buffers[0][...] = self.small[...]
        self.pair[-1][0].start()

    def begin(self, index):
        for copy in self.pair[index] or self.across[index]:
            copy.start()
        self.own[index].start()

    def first(self, index):
        mine, other = self.buffers[index][:2]
        groups = self.groups
        self.own[index].wait()
        if not self.pair[index]:
            return
        self.pair[index][0].wait_recv()

        def add(i, carry):
            at = (i // groups, i % groups)
            mine[at] = mine[at] + other[at]
            return carry

        lax.fori_loop(0, self.dp * groups, add, 0)
        for copy in self.across[index]:
            copy.start()

    def first_small(self):
        one, came, two = self.small_buffers[:3]
        self.pair[-1][0].wait_recv()
        two[...] = one[...] + came[...]
        for copy in self.across[-1]:
            copy.start()

    def middle(self, index):
        mine, _, came, sums, _ = self.buffers[index]
        for copy in self.across[index]:
            copy.wait_recv()

        def add(k, carry):
            total = mine[k, self.g].astype(F32)
            for j in range(self.groups - 1):
                total = total + came[j, k].astype(F32)
            sums[k] = total.astype(BF)
            return carry

        lax.fori_loop(0, self.dp, add, 0)
        for copy in self.along[index]:
            copy.start()

    def middle_small(self):
        _, _, two, groups_in, three, _ = self.small_buffers
        for copy in self.across[-1]:
            copy.wait_recv()
        total = two[...]
        for j in range(self.groups - 1):
            total = total + groups_in[j]
        three[...] = total
        for copy in self.along[-1]:
            copy.start()

    def finish(self):
        for index, out in enumerate(self.outs):
            sums, last = self.buffers[index][3:]
            for copy in self.along[index]:
                copy.wait_recv()
            total = sums[self.d].astype(F32)
            for j in range(self.dp - 1):
                total = total + last[j].astype(F32)
            out[...] = total
        three, dp_in = self.small_buffers[4:]
        for copy in self.along[-1]:
            copy.wait_recv()
        total = three[...]
        for j in range(self.dp - 1):
            total = total + dp_in[j]
        self.small_out[...] = total
        for batch in self.pair + self.across + self.along:
            for copy in batch:
                copy.wait_send()


class Exchange:
    def __init__(self, ctx, mover, source, target):
        d, c = lax.axis_index("dp"), lax.axis_index("ctx")
        groups = ctx // 2
        self.steps = []
        for t in range(groups):
            group = flip(c // 2, t, groups)
            same, other = group * 2 + c % 2, group * 2 + 1 - c % 2
            if t == 0:
                self.own = mover.local(source.at[c], target.at[c])
                batch = []
            else:
                batch = [mover.remote(source.at[same], target.at[c], (d, same))]
            batch.append(mover.remote(source.at[other], target.at[c], (d, other)))
            self.steps.append(batch)

    @staticmethod
    def count(ctx):
        return ctx - 1

    def start(self, t):
        if t == 0:
            self.own.start()
        for copy in self.steps[t]:
            copy.start()

    def arrive(self, t):
        if t == 0:
            self.own.wait()
        for copy in self.steps[t]:
            copy.wait_recv()

    def sent(self):
        for batch in self.steps:
            for copy in batch:
                copy.wait_send()


def columns(values):
    return jnp.sum(values, axis=0, keepdims=True)


def finish_kernel(dp, ctx, *refs):
    (xb, dq, dk, dv, w, grad_sum), refs = refs[:6], refs[6:]
    outs, small_out, x_out, refs = refs[:3], refs[3], refs[4], refs[5:]
    grads, result, small, refs = refs[:3], refs[3], refs[4], refs[5:]
    buffers, small_buffers, (local_sem, send_sem, recv_sem) = refs[:15], refs[15:21], refs[21:]
    d, c = lax.axis_index("dp"), lax.axis_index("ctx")
    groups = ctx // 2
    g = c // 2
    half, width = result.shape[1:]
    held = grads[0].shape[3]
    mover = Mover(local_sem, send_sem, recv_sem)
    scatter = Scatter(
        dp,
        ctx,
        grads,
        outs,
        [buffers[i * 5 : i * 5 + 5] for i in range(3)],
        small,
        small_out,
        small_buffers,
        mover,
    )
    give = Exchange(ctx, mover, result, x_out)
    greet([((d + k) % dp, c) for k in range(1, dp)] + [(d, (c + k) % ctx) for k in range(1, ctx)])
    small[...] = jnp.zeros_like(small)
    small[0:1, :] = columns(dq[...].astype(F32))
    small[1:2, :] = columns(dv[...].astype(F32))
    scatter.begin_small()

    across = xb[...].T

    def weight_gradient(index, rows_grad):
        total = dg(across, rows_grad[...], NN)
        for block in range(dp * ctx):
            at = (block // ctx, block % ctx // 2, block % 2)
            grads[index][at] = total[block * held : (block + 1) * held].astype(BF)
        scatter.begin(index)

    def row_tile(t):
        block = flip(g, t, groups)
        rows = pl.ds(pl.multiple_of(block * 2 * half, 2 * half), 2 * half)
        total = grad_sum[rows, :]
        for i, rows_grad in enumerate((dq, dk, dv)):
            total = total + dg(rows_grad[rows, :], w[:, i * width : (i + 1) * width], NT)
        result[pl.ds(block * 2, 2)] = total.astype(BF).reshape(2, half, width)
        give.start(t)

    tiles = list(range(groups - 1, -1, -1))
    for index, rows_grad in enumerate((dq, dk, dv)):
        weight_gradient(index, rows_grad)
        row_tile(tiles.pop(0))
        if index == 0:
            scatter.first_small()
        scatter.first(index)
    for t in tiles:
        row_tile(t)
    scatter.middle_small()
    for index in range(3):
        scatter.middle(index)
    scatter.finish()
    for t in range(groups):
        give.arrive(t)
    give.sent()


def finish_gradients(xb, dq, dk, dv, w, grad_sum, dp, ctx):
    rows, width = xb.shape
    remotes = Scatter.count(dp, ctx, 3) + Exchange.count(ctx)
    S = jax.ShapeDtypeStruct
    vmem = pl.BlockSpec(memory_space=pltpu.VMEM)
    source = S((dp, ctx // 2, 2, width // (dp * ctx), width), BF)
    small = S((8, width), F32)
    moved = (ctx, rows // ctx, width)
    return pl.pallas_call(
        functools.partial(finish_kernel, dp, ctx),
        in_specs=[vmem] * 6,
        out_specs=[vmem] * 4 + [pl.BlockSpec(memory_space=pl.ANY)],
        out_shape=[S(source.shape[3:], F32)] * 3 + [small, S(moved, BF)],
        scratch_shapes=[pltpu.VMEM(source.shape, BF)] * 3
        + [pltpu.VMEM(moved, BF), pltpu.VMEM(small.shape, F32)]
        + Scatter.scratch(dp, ctx, [source] * 3, small)
        + [
            pltpu.SemaphoreType.DMA((4,)),
            pltpu.SemaphoreType.DMA((remotes,)),
            pltpu.SemaphoreType.DMA((remotes,)),
        ],
        compiler_params=pltpu.CompilerParams(
            collective_id=3, has_side_effects=True, vmem_limit_bytes=VMEM_BYTES
        ),
        name="finish_gradients",
    )(xb, dq, dk, dv, w, grad_sum)


def head_lanes(shape, h):
    lane = lax.broadcasted_iota(jnp.int32, shape, len(shape) - 1)
    return (lane >= 64) == (h == 1), lane == (64 if h == 0 else 0)


def load_keys(keys, own_ref, sib_ref, lengths_ref, ctx):
    c = lax.axis_index("ctx")
    rows = own_ref.shape[0]
    half = rows // ctx
    length = lengths_ref[lax.axis_index("dp") * (ctx // 2) + c // 2]
    slot = lax.broadcasted_iota(jnp.int32, (rows, 128), 0)
    source = lax.broadcasted_iota(jnp.int32, (ctx, half, 128), 0).reshape(rows, 128)
    high = (2 * ctx - 1 - 2 * source) * half + slot
    for i, ref in enumerate((own_ref, sib_ref)):
        member = c % 2 if i == 0 else 1 - c % 2
        counted = jnp.where(member == 0, slot, high) < length
        for h in range(2):
            inside, spare = head_lanes((rows, 128), h)
            rest = jnp.where(spare & ~counted, masked_score, 0.0).astype(BF)
            keys[h, i * rows : (i + 1) * rows, :] = jnp.where(inside, ref[...], rest)


def forward_kernel(dp, ctx, bq, *refs):
    (x_ref, w_ref, vec_ref, lengths_ref), gathered, refs = refs[:4], refs[4:7], refs[7:]
    (mb_ref, mix_ref, lse_ref, own_to, sib_to), spread_to, refs = refs[:5], refs[5:8], refs[8:]
    keys, own, sib, local_sem, send_sem, recv_sem, pair_send, pair_recv, store_sem = refs
    spread = Spread(dp, ctx, gathered, spread_to, Mover(local_sem, send_sem, recv_sem))
    pairs, steps = pl.num_programs(0), pl.num_programs(1)
    pair, j = pl.program_id(0), pl.program_id(1)
    step = pair * steps + j
    last = forward_steps(pairs, steps)
    half, width = x_ref.shape

    def to_sibling(number):
        return pltpu.make_async_remote_copy(
            src_ref=own.at[number, pl.ds(1, 2)],
            dst_ref=sib.at[number],
            send_sem=pair_send.at[number],
            recv_sem=pair_recv.at[number],
            device_id=spread.devices[-1],
            device_id_type=MESH,
        )

    def stores(number):
        return [
            pltpu.make_async_copy(own.at[number], own_to.at[number], store_sem.at[number, 0]),
            pltpu.make_async_copy(sib.at[number], sib_to.at[number], store_sem.at[number, 1]),
        ]

    def project(number):
        lanes = [pl.ds(pl.multiple_of(number * 128 + i * width, 128), 128) for i in range(3)]
        weights = jnp.concatenate([w_ref[:, part] for part in lanes], axis=1)
        rows = dg(x_ref[...], weights, NN)
        own[number, 0] = (rows[:, :128] + vec_ref[0:1, lanes[0]]).astype(BF)
        own[number, 1] = rows[:, 128:256].astype(BF)
        own[number, 2] = (rows[:, 256:] + vec_ref[1:2, lanes[0]]).astype(BF)
        to_sibling(number).start()

    @pl.when(step == 0)
    def _():
        spread.begin()
        project(pair)

    @pl.when(j == 0)
    def _():
        to_sibling(pair).wait_recv()
        for copy in stores(pair):
            copy.start()
        load_keys(keys, own.at[pair, 1], sib.at[pair, 0], lengths_ref, ctx)

    @pl.when((j == 1) & (pair < pairs - 1))
    def _():
        project(pair + 1)

    rows = pl.ds(pl.multiple_of(j * bq, bq), bq)
    q = own[pair, 0, rows, :] * jnp.asarray(0.125, BF)
    scores = []
    for h in range(2):
        inside, spare = head_lanes((bq, 128), h)
        rest = jnp.where(spare, jnp.ones((), BF), jnp.zeros((), BF))
        scores.append(dg(jnp.where(inside, q, rest), keys[h], NT))
    outs, lses = [], []
    for h in range(2):
        top = jnp.max(scores[h], axis=1, keepdims=True)
        weights = jnp.exp(scores[h] - top)
        total = jnp.sum(weights, axis=1, keepdims=True)
        low = weights.astype(BF)
        mixed = dg(low[:, :half], own[pair, 2], NN) + dg(low[:, half:], sib[pair, 1], NN)
        outs.append(mixed / total)
        lses.append(top + jnp.log(total))
    lane = lax.broadcasted_iota(jnp.int32, (bq, 128), 1)
    mixed = jnp.where(lane < 64, outs[0], outs[1])
    mix_ref[...] = mixed
    mb_ref[...] = mixed.astype(BF)
    lse_ref[0] = jnp.where(lane == 0, lses[0], lses[1]).T[:8]

    for index, at in enumerate(last):

        @pl.when(step == at)
        def _(index=index):
            spread.forward(index)

    @pl.when(step == last[-1])
    def _():
        spread.finish()
        for number in range(pairs):
            to_sibling(number).wait_send()
            for copy in stores(number):
                copy.wait()


def attention_forward(x, w, vec, lengths, gathered, dp, ctx, bq=256):
    rows, width = x.shape
    pairs = width // 128
    S = jax.ShapeDtypeStruct
    blk = pl.BlockSpec((bq, 128), lambda p, j: (j, p))
    any_space = pl.BlockSpec(memory_space=pl.ANY)
    vmem = pl.BlockSpec(memory_space=pltpu.VMEM)
    remotes = Spread.count(ctx // 2, 3)
    return pl.pallas_call(
        functools.partial(forward_kernel, dp, ctx, bq),
        grid=(pairs, rows // bq),
        in_specs=[vmem] * 3 + [pl.BlockSpec(memory_space=pltpu.SMEM)] + [any_space] * 3,
        out_specs=[blk, blk, pl.BlockSpec((1, 8, bq), lambda p, j: (p, 0, j))] + [any_space] * 5,
        out_shape=[S(x.shape, BF), S(x.shape, F32), S((pairs, 8, rows), F32)]
        + [S((pairs, count, rows, 128), BF) for count in (3, 2)]
        + [S((dp, ctx) + array.shape[1:], BF) for array in gathered],
        scratch_shapes=[
            pltpu.VMEM((2, 2 * rows, 128), BF),
            pltpu.VMEM((pairs, 3, rows, 128), BF),
            pltpu.VMEM((pairs, 2, rows, 128), BF),
            pltpu.SemaphoreType.DMA((3,)),
            pltpu.SemaphoreType.DMA((remotes,)),
            pltpu.SemaphoreType.DMA((remotes,)),
            pltpu.SemaphoreType.DMA((pairs,)),
            pltpu.SemaphoreType.DMA((pairs,)),
            pltpu.SemaphoreType.DMA((pairs, 2)),
        ],
        compiler_params=pltpu.CompilerParams(
            vmem_limit_bytes=VMEM_BYTES, collective_id=1, has_side_effects=True
        ),
        cost_estimate=pl.CostEstimate(
            flops=16 * rows * rows * 128 * pairs,
            bytes_accessed=14 * rows * 768,
            transcendentals=4 * rows * rows * pairs,
        ),
        name="attend",
    )(x, w, vec, lengths, *gathered)


def forward_steps(pairs, steps):
    count = pairs * steps
    return (count * 5 // 24, count * 15 // 24, count - 1)


def backward_steps(pairs, steps):
    count = pairs * steps
    first = [count * at // 12 for at in (0, 0, 1)]
    middle = [count * at // 12 for at in (5, 4, 8)]
    return first, middle


def backward_kernel(dp, ctx, ck, *refs):
    (q_ref, ko_ref, vo_ref, ks_ref, vs_ref, do_ref, mix_ref, lengths_ref, lse_ref), refs = (
        refs[:9],
        refs[9:],
    )
    q_ref, ko_ref, vo_ref, ks_ref, vs_ref = (
        ref.at[0, 0] for ref in (q_ref, ko_ref, vo_ref, ks_ref, vs_ref)
    )
    sources, small, refs = refs[:3], refs[3], refs[4:]
    (dq_ref, dk_ref, dv_ref), refs = refs[:3], refs[3:]
    summed, small_out, refs = refs[:3], refs[3], refs[4:]
    (keys, dk, dv, held, going, coming), refs = refs[:6], refs[6:]
    buffers, small_buffers, refs = refs[:15], refs[15:21], refs[21:]
    local_sem, send_sem, recv_sem, pair_send, pair_recv = refs
    scatter = Scatter(
        dp,
        ctx,
        sources,
        summed,
        [buffers[i * 5 : i * 5 + 5] for i in range(3)],
        small,
        small_out,
        small_buffers,
        Mover(local_sem, send_sem, recv_sem),
    )
    steps = pl.num_programs(1)
    j = pl.program_id(1)
    step = pl.program_id(0) * steps + j

    pair = pl.program_id(0)
    sibling = scatter.devices[-1]

    def to_sibling(number):
        return [
            pltpu.make_async_remote_copy(
                src_ref=going.at[number, i],
                dst_ref=coming.at[number, i],
                send_sem=pair_send.at[number * 2 + i],
                recv_sem=pair_recv.at[number * 2 + i],
                device_id=sibling,
                device_id_type=MESH,
            )
            for i in range(2)
        ]

    def settle(number):
        lanes = pl.ds(pl.multiple_of(number * 128, 128), 128)
        for i, (copy, out) in enumerate(zip(to_sibling(number), (dk_ref, dv_ref))):
            copy.wait_recv()
            total = held[number % 2, i] + coming[number, i].astype(F32)
            out[:, lanes] = total.astype(BF)

    @pl.when(step == 0)
    def _():
        greet(scatter.devices)
        scatter.begin(1)
        scatter.begin_small()
        scatter.begin(0)
        scatter.begin(2)

    @pl.when((j == 0) & (pair > 0))
    def _():
        settle(pair - 1)

    @pl.when(j == 0)
    def _():
        load_keys(keys, ko_ref, ks_ref, lengths_ref, ctx)
        dk[...] = jnp.zeros_like(dk)
        dv[...] = jnp.zeros_like(dv)

    half, bq = ko_ref.shape[0], q_ref.shape[0]
    q = q_ref[...] * jnp.asarray(0.125, BF)
    do = do_ref[...]
    prod = (do.astype(F32) * mix_ref[...]).T
    zero, one = jnp.zeros((), BF), jnp.ones((), BF)
    heads = []
    for h in range(2):
        inside, spare = head_lanes((bq, 128), h)
        heads.append(
            (
                jnp.where(inside, q, jnp.where(spare, one, zero)),
                jnp.where(inside, q, zero),
                jnp.where(inside, do, zero),
                lse_ref[0, h : h + 1, :],
                jnp.sum(prod[h * 64 : (h + 1) * 64], axis=0, keepdims=True),
            )
        )
    dq = jnp.zeros((bq, 128), F32)
    for first in range(0, 2 * half, ck):
        rows = slice(first, first + ck)
        v = vo_ref[rows, :] if first < half else vs_ref[first - half : first - half + ck, :]
        for h in range(2):
            qm, qz, dom, lse, delta = heads[h]
            k = keys[h, rows, :]
            p = jnp.exp(dg(k, qm, NT) - lse)
            ds = (p * (dg(v, dom, NT) - delta)).astype(BF)
            dv[rows, :] += dg(p.astype(BF), dom, NN)
            dk[rows, :] += dg(ds, qz, NN)
            dq = dq + dg(ds, k, TN)
    dq_ref[...] = (dq * 0.125).astype(BF)

    @pl.when(j == steps - 1)
    def _():
        for i, total in enumerate((dk, dv)):
            held[pair % 2, i] = total[:half, :]
            going[pair, i] = total[half:, :].astype(BF)
        for copy in to_sibling(pair):
            copy.start()

    first, middle_at = backward_steps(pl.num_programs(0), steps)

    @pl.when(step == first[0])
    def _():
        scatter.first_small()

    @pl.when(step == middle_at[0])
    def _():
        scatter.middle_small()

    for index in range(3):

        @pl.when(step == first[index])
        def _(index=index):
            scatter.first(index)

        @pl.when(step == middle_at[index])
        def _(index=index):
            scatter.middle(index)

    @pl.when(step == pl.num_programs(0) * steps - 1)
    def _():
        scatter.finish()
        settle(pair)
        for number in range(pl.num_programs(0)):
            for copy in to_sibling(number):
                copy.wait_send()


def attention_backward(own, sib, do, mix, lengths, lse, sources, small, dp, ctx, bq=512, ck=512):
    rows, width = do.shape
    pairs = width // 128
    S = jax.ShapeDtypeStruct
    blk = pl.BlockSpec((bq, 128), lambda p, j: (j, p))
    whole_of = [
        pl.BlockSpec((1, 1, rows, 128), lambda p, j, i=i: (p, i, 0, 0)) for i in (1, 2, 0, 1)
    ]
    any_space = pl.BlockSpec(memory_space=pl.ANY)
    remotes = Scatter.count(dp, ctx, 3)
    whole = pl.BlockSpec(small.shape, lambda p, j: (0, 0))
    sums = [s.shape[-2:] for s in sources]
    all_rows = pl.BlockSpec((rows, width), lambda p, j: (0, 0))
    return pl.pallas_call(
        functools.partial(backward_kernel, dp, ctx, ck),
        grid=(pairs, rows // bq),
        in_specs=[pl.BlockSpec((1, 1, bq, 128), lambda p, j: (p, 0, j, 0))]
        + whole_of
        + [blk, blk]
        + [pl.BlockSpec(memory_space=pltpu.SMEM)]
        + [pl.BlockSpec((1, 8, bq), lambda p, j: (p, 0, j))]
        + [any_space] * 3
        + [whole],
        out_specs=[blk, all_rows, all_rows]
        + [pl.BlockSpec(shape, lambda p, j: (0, 0)) for shape in sums]
        + [whole],
        out_shape=[S(do.shape, BF)] * 3
        + [S(shape, F32) for shape in sums]
        + [S(small.shape, F32)],
        scratch_shapes=[
            pltpu.VMEM((2, 2 * rows, 128), BF),
            pltpu.VMEM((2 * rows, 128), F32),
            pltpu.VMEM((2 * rows, 128), F32),
            pltpu.VMEM((2, 2, rows, 128), F32),
            pltpu.VMEM((pairs, 2, rows, 128), BF),
            pltpu.VMEM((pairs, 2, rows, 128), BF),
        ]
        + Scatter.scratch(dp, ctx, sources, small)
        + [
            pltpu.SemaphoreType.DMA((3,)),
            pltpu.SemaphoreType.DMA((remotes,)),
            pltpu.SemaphoreType.DMA((remotes,)),
            pltpu.SemaphoreType.DMA((2 * pairs,)),
            pltpu.SemaphoreType.DMA((2 * pairs,)),
        ],
        compiler_params=pltpu.CompilerParams(
            vmem_limit_bytes=VMEM_BYTES, collective_id=2, has_side_effects=True
        ),
        cost_estimate=pl.CostEstimate(
            flops=40 * rows * rows * 128 * pairs,
            bytes_accessed=26 * rows * 768,
            transcendentals=4 * rows * rows * pairs,
        ),
        name="attend_back",
    )(own, own, own, sib, sib, do, mix, lengths, lse, *sources, small)


def gelu_and_slope(x):
    t = 1.0 / (1.0 + 0.2316419 * jnp.abs(x))
    bell = 0.3989422804 * jnp.exp(-0.5 * x * x)
    poly = 1.330274429 * t - 1.821255978
    poly = poly * t + 1.781477937
    poly = poly * t - 0.356563782
    poly = poly * t + 0.319381530
    tail = bell * (poly * t)
    below = jnp.where(x < 0.0, tail, 1.0 - tail)
    return x * below, below + x * bell


def middle_kernel(dp, ctx, *refs):
    (mb, xb, rest_src, up_src, vec, bias_up, wo_src, wu_src, wd_src), refs = refs[:9], refs[9:]
    (dm, grad_sum, out_to, go_to, gu_to, gd_to, small), refs = refs[:7], refs[7:]
    (wo, wu, wd, rest, upstream, result, active, dinner, slope, fb, db, da), refs = (
        refs[:12],
        refs[12:],
    )
    (other, summed), refs = refs[:2], refs[2:]
    load_sem, local_sem, send_sem, recv_sem = refs
    groups = ctx // 2
    g = lax.axis_index("ctx") // 2
    half, width = result.shape[1:]
    tile = 2 * half
    chunks = range(wu.shape[1] // width)
    step = pl.program_id(0)
    mover = Mover(local_sem, send_sem, recv_sem)
    rest_in = Exchange(ctx, mover, rest_src, rest)
    up_in = Exchange(ctx, mover, up_src, upstream)
    give = Exchange(ctx, mover, result, out_to)
    loads = [
        pltpu.make_async_copy(source, target, load_sem.at[i])
        for i, (source, target) in enumerate(((wo_src, wo), (wu_src, wu), (wd_src, wd)))
    ]
    stores = [
        pltpu.make_async_copy(source, target, load_sem.at[i])
        for i, (source, target) in enumerate(((wo, go_to), (wu, gu_to), (summed, gd_to)))
    ]
    d, c = lax.axis_index("dp"), lax.axis_index("ctx")
    held = other.shape[2]

    def block_rows(i, k, member):
        return pl.ds(pl.multiple_of(((i * groups + k) * 2 + member) * held, 8), held)

    blocks = [(i, k) for i in range(dp) for k in range(groups)]
    to_sibling = [
        mover.remote(wd.at[block_rows(i, k, 1 - c % 2)], other.at[i, k], (d, g * 2 + 1 - c % 2))
        for i, k in blocks
    ]

    def load(index):
        @pl.when(step == 0)
        def _():
            loads[index].wait()

    @pl.when(step == 0)
    def _():
        for copy in loads:
            copy.start()
        greet([(d, (c + k) % ctx) for k in range(1, ctx)])
        for t in range(groups):
            rest_in.start(t)
            up_in.start(t)
        small[...] = jnp.zeros_like(small)

    @pl.when(step < groups)
    def _():
        block = flip(g, step, groups)
        rows = pl.ds(pl.multiple_of(block * tile, tile), tile)
        pair = pl.ds(block * 2, 2)
        load(0)
        hidden = dg(mb[rows, :], wo[...], NN) + vec[2:3, :] + xb[rows, :].astype(F32)
        for t in range(groups):

            @pl.when(step == t)
            def _(t=t):
                rest_in.arrive(t)

        hidden = hidden + rest[pair].reshape(tile, width).astype(F32)
        normed, standard_one, inverse_one = normalize(hidden, vec[6:7, :], vec[4:5, :])
        low = normed.astype(BF)
        fb[rows, :] = low
        load(1)
        parts = [slice(i * width, (i + 1) * width) for i in chunks]
        inner = dg(low, wu[:, parts[0]], NN)
        for i, part in enumerate(parts):
            ahead = dg(low, wu[:, parts[i + 1]], NN) if i + 1 < len(parts) else None
            value, slope[:, part] = gelu_and_slope(inner + bias_up[:, part])
            active[rows, part] = value.astype(BF)
            inner = ahead
        load(2)
        hidden = normed + dg(active[rows, :], wd[...], NN) + vec[3:4, :]
        out, standard, inverse = normalize(hidden, vec[7:8, :], vec[5:6, :])
        result[pair] = out.astype(BF).reshape(2, half, width)
        for t in range(groups):

            @pl.when(step == t)
            def _(t=t):
                give.start(t)
                up_in.arrive(t)

        error = upstream[pair].reshape(tile, width).astype(F32)
        grad = normalize_back(error, standard, inverse, vec[7:8, :])
        low_grad = grad.astype(BF)
        db[rows, :] = low_grad
        small[1:2, :] += columns(low_grad.astype(F32))
        small[3:4, :] += columns(error)
        small[5:6, :] += columns(error * standard)
        for i in chunks:
            part = slice(i * width, (i + 1) * width)
            change = dg(low_grad, wd[part, :], NT) * slope[:, part]
            change = change.astype(BF)
            dinner[rows, part] = change
            small[6 + i : 7 + i, :] += columns(change.astype(F32))
        grad = grad + dg(dinner[rows, :], wu[...], NT)
        small[2:3, :] += columns(grad)
        small[4:5, :] += columns(grad * standard_one)
        grad = normalize_back(grad, standard_one, inverse_one, vec[6:7, :])
        grad_sum[rows, :] = grad
        low_grad = grad.astype(BF)
        da[rows, :] = low_grad
        small[0:1, :] += columns(low_grad.astype(F32))
        dm[rows, :] = dg(low_grad, wo[...], NT).astype(BF)

    @pl.when(step == groups)
    def _():
        for i in chunks:
            part = slice(i * width, (i + 1) * width)
            wd[part, :] = dg(active[:, part], db[...], TN).astype(BF)
        for copy in to_sibling:
            copy.start()
        across = fb[...].T
        for i in chunks:
            part = slice(i * width, (i + 1) * width)
            wu[:, part] = dg(across, dinner[:, part], NN).astype(BF)
        stores[1].start()
        for copy in to_sibling:
            copy.wait()
        for i, k in blocks:
            summed[i, k] = wd[block_rows(i, k, c % 2), :] + other[i, k]
        stores[2].start()
        wo[...] = dg(mb[...], da[...], TN).astype(BF)
        stores[0].start()
        for t in range(groups):
            give.arrive(t)
        for move in (rest_in, up_in, give):
            move.sent()
        for copy in stores:
            copy.wait()


def middle(mb, xb, rest, upstream, vec, bias_up, wo, wu, wd, dp, ctx):
    rows, width = mb.shape
    hidden = wu.shape[1]
    half = rows // ctx
    S = jax.ShapeDtypeStruct
    any_space = pl.BlockSpec(memory_space=pl.ANY)
    vmem = pl.BlockSpec(memory_space=pltpu.VMEM)
    held = (dp, ctx // 2, hidden // (dp * ctx), width)
    remotes = 3 * Exchange.count(ctx) + dp * (ctx // 2)
    return pl.pallas_call(
        functools.partial(middle_kernel, dp, ctx),
        grid=(ctx // 2 + 1,),
        in_specs=[vmem, vmem, any_space, any_space, vmem, vmem] + [any_space] * 3,
        out_specs=[vmem, vmem] + [any_space] * 4 + [vmem],
        out_shape=[S(mb.shape, BF), S(mb.shape, F32), S(rest.shape, BF)]
        + [S(wo.shape, BF), S(wu.shape, BF), S(held, BF)]
        + [S((16, width), F32)],
        scratch_shapes=[pltpu.VMEM(array.shape, BF) for array in (wo, wu, wd)]
        + [pltpu.VMEM(rest.shape, BF)] * 3
        + [pltpu.VMEM((rows, hidden), BF)] * 2
        + [pltpu.VMEM((2 * half, hidden), F32)]
        + [pltpu.VMEM((rows, width), BF)] * 3
        + [pltpu.VMEM(held, BF)] * 2
        + [
            pltpu.SemaphoreType.DMA((3,)),
            pltpu.SemaphoreType.DMA((3,)),
            pltpu.SemaphoreType.DMA((remotes,)),
            pltpu.SemaphoreType.DMA((remotes,)),
        ],
        compiler_params=pltpu.CompilerParams(
            vmem_limit_bytes=VMEM_BYTES, collective_id=4, has_side_effects=True
        ),
        cost_estimate=pl.CostEstimate(
            flops=2 * 3 * rows * width * (2 * hidden + width),
            bytes_accessed=50 << 20,
            transcendentals=rows * hidden,
        ),
        name="middle",
    )(mb, xb, rest, upstream, vec, bias_up, wo, wu, wd)


def normalize(hidden, scale_row, shift_row):
    centred = hidden - jnp.mean(hidden, axis=-1, keepdims=True)
    inverse = lax.rsqrt(jnp.mean(centred * centred, axis=-1, keepdims=True) + epsilon)
    standard = centred * inverse
    return (standard * scale_row + shift_row, standard, inverse)


def normalize_back(gradient, standard, inverse, scale_row):
    scaled = gradient * scale_row
    centred = scaled - jnp.mean(scaled, axis=-1, keepdims=True)
    return (centred - standard * jnp.mean(scaled * standard, axis=-1, keepdims=True)) * inverse


def write_kernel(dp, ctx, small_ref, sums_ref, out_ref, tokens_ref, *refs):
    sources, (out_to, tokens_to), refs = refs[:6], refs[6:8], refs[8:]
    targets, (vectors_to, bias_to) = refs[:6], refs[6:]
    out_to[...] = out_ref[...].astype(F32)
    tokens_to[...] = tokens_ref[...].astype(F32)

    @pl.when(pl.program_id(0) == 0)
    def _():
        for source, target in zip(sources, targets):
            target[...] = source[...]
        device = lax.axis_index("dp") * ctx + lax.axis_index("ctx")
        width = small_ref.shape[1]
        held, held_up = vectors_to.shape[1], bias_to.shape[1]
        rows = jnp.concatenate([sums_ref[0:2, :], small_ref[0:6, :]], axis=0)
        vectors_to[...] = pltpu.roll(rows, (width - device * held) % width, 1)[:, :held]
        first = device * held_up
        row = small_ref[pl.ds(6 + first // width, 1), :]
        row = jnp.broadcast_to(row, (8, width))
        bias_to[...] = pltpu.roll(row, (width - first % width) % width, 1)[0:1, :held_up]


def write_out(small, sums, out, tokens, own, held_up, dp, ctx):
    block = pl.BlockSpec((1,) + out.shape[1:], lambda i: (i, 0, 0))
    S = jax.ShapeDtypeStruct

    def whole(shape):
        return pl.BlockSpec(shape, lambda i: (0, 0))

    shapes = [array.shape for array in own]
    vectors = (8, out.shape[2] // (dp * ctx))
    return pl.pallas_call(
        functools.partial(write_kernel, dp, ctx),
        grid=(ctx,),
        in_specs=[whole(small.shape), whole(sums.shape), block, block]
        + [whole(shape) for shape in shapes],
        out_specs=[block, block]
        + [whole(shape) for shape in shapes]
        + [whole(vectors), whole((1, held_up))],
        out_shape=[S(out.shape, F32)] * 2
        + [S(shape, F32) for shape in shapes]
        + [S(vectors, F32), S((1, held_up), F32)],
        compiler_params=pltpu.CompilerParams(vmem_limit_bytes=VMEM_BYTES),
        name="write_out",
    )(small, sums, out, tokens, *own)


def on_device(
    tokens, cotangent, lengths, w_query, w_key, w_value, w_attn_out, w_up, b_up, w_down, vectors
):
    seqs, rows_dev, width = tokens.shape
    dp = lax.axis_size("dp")
    ctx = lax.axis_size("ctx")
    half = rows_dev // 2
    rows = half * ctx
    def by_owner(grad):
        return grad.reshape(dp, ctx // 2, 2, -1, grad.shape[1])

    split = tokens.reshape(ctx, half, width)
    held = w_query.shape[0]
    extra = jnp.concatenate([vectors.T, b_up.reshape(held, -1)], axis=1)
    extra = jnp.pad(extra, ((0, 0), (0, 128 - extra.shape[1])))
    low_in, left_out, upstream, full_first, *over_dp = gather_first(
        split,
        cotangent.reshape(ctx, half, width),
        jnp.concatenate([w_query, w_key, w_value, extra], axis=1),
        w_attn_out,
        w_up,
        w_down,
        dp,
        ctx,
    )
    low_in = low_in.reshape(rows, width)
    full_first = full_first.reshape(width, -1)
    vector_rows = full_first[:, 3 * width : 3 * width + 8].T.astype(F32)
    bias_columns = b_up.shape[0] // held
    full_bias_up = full_first[:, 3 * width + 8 : 3 * width + 8 + bias_columns].reshape(-1).astype(F32)
    low_mixed, mixed, lse, own, sib, full_attn, full_up, full_down = attention_forward(
        low_in, full_first, vector_rows, lengths, over_dp, dp, ctx
    )
    full_attn = full_attn.reshape(width, width)
    full_up = full_up.reshape(width, -1)
    full_down = full_down.reshape(-1, width)

    d_mixed, grad_sum, result, d_attn, d_up, part_down, small = middle(
        low_mixed,
        low_in,
        left_out,
        upstream,
        vector_rows,
        full_bias_up.reshape(1, -1),
        full_attn,
        full_up,
        full_down,
        dp,
        ctx,
    )
    dq, dk, dv, own_attn, own_down, own_up, small = attention_backward(
        own,
        sib,
        d_mixed,
        mixed,
        lengths,
        lse,
        [by_owner(d_attn), part_down, by_owner(d_up)],
        small,
        dp,
        ctx,
    )
    own_query, own_key, own_value, sums, grad_tokens = finish_gradients(
        low_in, dq, dk, dv, full_first, grad_sum, dp, ctx
    )
    output, grad_tokens, *own, own_vectors, own_bias_up = write_out(
        small,
        sums,
        result,
        grad_tokens,
        [own_query, own_key, own_value, own_attn, own_up, own_down],
        b_up.shape[0],
        dp,
        ctx,
    )
    own_query, own_key, own_value, own_attn, own_up, own_down = own
    output = output.reshape(seqs, rows_dev, width)
    grad_tokens = grad_tokens.reshape(seqs, rows_dev, width)
    own_bias_up = own_bias_up.reshape(-1)
    return (
        output,
        grad_tokens,
        own_query,
        own_key,
        own_value,
        own_attn,
        own_up,
        own_bias_up,
        own_down,
        own_vectors,
    )


def solution(mesh):
    in_specs = (
        P("dp", "ctx", None),
        P("dp", "ctx", None),
        P(),
        P(("dp", "ctx"), None),
        P(("dp", "ctx"), None),
        P(("dp", "ctx"), None),
        P(("dp", "ctx"), None),
        P(("dp", "ctx"), None),
        P(("dp", "ctx")),
        P(("dp", "ctx"), None),
        P(None, ("dp", "ctx")),
    )
    out_specs = (
        P("dp", "ctx", None),
        P("dp", "ctx", None),
        P(("dp", "ctx"), None),
        P(("dp", "ctx"), None),
        P(("dp", "ctx"), None),
        P(("dp", "ctx"), None),
        P(("dp", "ctx"), None),
        P(("dp", "ctx")),
        P(("dp", "ctx"), None),
        P(None, ("dp", "ctx")),
    )
    return jax.shard_map(
        on_device, mesh=mesh, in_specs=in_specs, out_specs=out_specs, check_vma=False
    )
```

profile of v0, /device:TPU:1, one launch (start us, length us, event | category | flops | bytes accessed | tf_op | source)
XLA Modules:
  0.0 354.8 jit_solution(4879197396232189455)
XLA Ops:
  0.6 0.7 reshape.75
  1.4 0.8 copy.24
  2.2 0.1 fusion.2
  2.2 1.5 pad_maximum_fusion.refs_2_
  3.7 47.7 %gather_first.1 = (bf16[8,128,768]{2,1,0:T(8,128)(2,1)}, bf16[8,128,768]{2,1,0:T(8,128)(2,1)}, bf16[8,128,768]{2,1,0:T(8,128)(2,1)}, bf16[4,8,24,2432]{3,2,1,0:T...) custom-call(f32[8,128,768]{2,1,0:T(8,128)} %bitcast.19, ...), custom_call_target="tpu_custom_call" | custom-call | tf_op jit(solution)/shard_map/gather_first/pallas_call | solution.py:149
  51.4 1.0 slice_convert_fusion
  52.4 0.9 reshape.86.refs_5_
  53.3 1.0 convert_bitcast_fusion
  54.3 0.7 copy.25.refs_2_.refs_4_
  55.0 67.0 %attend.1 = (bf16[1024,768]{1,0:T(8,128)(2,1)}, f32[1024,768]{1,0:T(8,128)}, f32[6,8,1024]{2,1,0:T(8,128)}, bf16[6,3,1024,128]{3,2,1,0:T(8,128)(2,1)}, bf16[6,2,...) custom-call(bf16[1024,768]{1,0:T(8,128)(2,1)} %bitcast.21, ...), custom_call_target="tpu_custom_call" | custom-call | flops 12884901888 | bytes 11010048 | tf_op jit(solution)/shard_map/attend/pallas_call | solution.py:611
  122.0 78.9 %middle.1 = (bf16[1024,768]{1,0:T(8,128)(2,1)}, f32[1024,768]{1,0:T(8,128)}, bf16[8,128,768]{2,1,0:T(8,128)(2,1)}, bf16[768,768]{1,0:T(8,128)(2,1)}, bf16[768,30...) custom-call(bf16[1024,768]{1,0:T(8,128)(2,1)} %get-tuple-element.61.refs_0_, ...), custom_call_target="tpu_custom_call" | custom-call | flops 32614907904 | bytes 52428800 | tf_op jit(solution)/shard_map/middle/pallas_call | solution.py:1010
  201.0 90.9 %attend_back.1 = (bf16[1024,768]{1,0:T(8,128)(2,1)}, bf16[1024,768]{1,0:T(8,128)(2,1)}, bf16[1024,768]{1,0:T(8,128)(2,1)}, f32[24,768]{1,0:T(8,128)}, f32[96,768...) custom-call(bf16[6,3,1024,128]{3,2,1,0:T(8,128)(2,1)} %get-tuple-element.59.refs_0_.refs_1_.refs_2_, ...), custom_call_target="tpu_custom_call" | custom-call | flops 32212254720 | bytes 20447232 | tf_op jit(solution)/shard_map/attend_back/pallas_call | solution.py:805
  291.9 54.6 %finish_gradients.1 = (f32[24,768]{1,0:T(8,128)}, f32[24,768]{1,0:T(8,128)}, f32[24,768]{1,0:T(8,128)}, f32[8,768]{1,0:T(8,128)}, bf16[8,128,768]{2,1,0:T(8,128)(2,1)}) custom-call(bf16[1024,768]{1,0:T(8,128)(2,1)} %bitcast.23, bf16[1024,768]{1,0:T(8,128)(2,1)} %get-tuple-element.75.refs_1_, bf16[1024,768]{1,0:T(8,128)(2,1)} %get-tuple-element.76.refs_2_, ...), custom_call_target="tpu_custom_call" | custom-call | tf_op jit(solution)/shard_map/finish_gradients/pallas_call | solution.py:472
  346.6 7.8 %write_out.1 = (f32[8,128,768]{2,1,0:T(8,128)}, f32[8,128,768]{2,1,0:T(8,128)}, f32[24,768]{1,0:T(8,128)}, f32[24,768]{1,0:T(8,128)}, f32[24,768]{1,0:T(8,128)},...) custom-call(f32[16,768]{1,0:T(8,128)} %get-tuple-element.74.small_ref, ...), custom_call_target="tpu_custom_call" | custom-call | tf_op jit(solution)/shard_map/write_out/pallas_call | solution.py:1085
where the time goes:
time: 360 us; the launch traced here: 355 us
  Pallas kernels  347 us (96%)
    pallas_call x1, Pallas kernels, attention_backward(): pl.pallas_call(functools.partial(backward_kernel, dp, ctx, ck), grid=(pai...  90.9 us
    pallas_call x1, Pallas kernels, middle(): pl.pallas_call(functools.partial(middle_kernel, dp, ctx), grid=(ctx // 2...  78.9 us
    pallas_call x1, Pallas kernels, attention_forward(): pl.pallas_call(functools.partial(forward_kernel, dp, ctx, bq), grid=(pair...  67 us
    pallas_call x1, Pallas kernels, finish_gradients(): pl.pallas_call(functools.partial(finish_kernel, dp, ctx), in_specs=[vmem]...  54.6 us
    pallas_call x1, Pallas kernels, gather_first(): pl.pallas_call(functools.partial(gather_kernel, dp, ctx), in_specs=[any_s...  47.7 us
    pallas_call x1, Pallas kernels, write_out(): pl.pallas_call(functools.partial(write_kernel, dp, ctx), grid=(ctx,), in_...  7.78 us

commit v1 on v0

--- a/solution.py
+++ b/solution.py
@@ -69,6 +69,65 @@
         total = total + (group // bit + step // bit) % 2 * bit
         bit *= 2
     return total
+
+
+class Spread:
+    def __init__(self, dp, ctx, sources, targets, mover):
+        d, c, g, m, over_dp, over_groups, sibling = place(dp, ctx)
+        groups = ctx // 2
+        bits = [1 << i for i in range(groups.bit_length() - 1)]
+        self.levels = len(bits)
+        self.devices = [(d, flip(g, bit, groups) * 2 + m) for bit in bits] + [sibling]
+        self.own, self.copies, self.onward = [], [], []
+        for source, target in zip(sources, targets):
+
+            def column(mask):
+                return flip(g, mask, groups) * 2 + m
+
+            self.own.append([] if source is None else [mover.local(source, target.at[:, c])])
+            source = target.at[:, c] if source is None else source
+            copies = [[] for _ in range(self.levels + 1)]
+            for start, order in ((0, bits), (dp // 2, bits[::-1])):
+                part = pl.ds(start, dp // 2)
+                for i, bit in enumerate(order):
+                    for mask in range(groups):
+                        if any(mask & other for other in order[i:]):
+                            continue
+                        place_in = target.at[part, column(mask)]
+                        copies[bin(mask).count("1")].append(
+                            mover.remote(
+                                place_in if mask else source.at[part], place_in, (d, column(bit))
+                            )
+                        )
+            self.copies.append(copies)
+            onward = [[mover.remote(source, target.at[:, c], sibling)]]
+            onward += [[] for _ in range(self.levels)]
+            for mask in range(1, groups):
+                block = target.at[:, column(mask)]
+                onward[bin(mask).count("1")].append(mover.remote(block, block, sibling))
+            self.onward.append(onward)
+
+    @staticmethod
+    def count(ctx, arrays):
+        return arrays * (2 * (ctx // 2 - 1) + ctx // 2)
+
+    def begin(self):
+        for own, copies, onward in zip(self.own, self.copies, self.onward):
+            for copy in copies[0] + own + onward[0]:
+                copy.start()
+
+    def forward(self, index, level):
+        for copy in self.copies[index][level - 1]:
+            copy.wait_recv()
+        for copy in self.copies[index][level] + self.onward[index][level]:
+            copy.start()
+
+    def finish(self):
+        for own, copies, onward in zip(self.own, self.copies, self.onward):
+            for copy in own + sum(onward, []):
+                copy.wait()
+            for copy in sum(copies, []):
+                copy.wait_send()
 
 
 def gather_kernel(dp, ctx, *refs):
@@ -97,7 +156,6 @@
         )
     ]
     along = [mover.remote(w, w_full.at[d, c], device) for device in over_dp]
-    across = [[mover.remote(w, w_full.at[d, c], device) for device in over_groups]]
     rows = [
         mover.remote(x.at[(c + k) % ctx], x_in.at[c], (d, (c + k) % ctx)) for k in range(1, ctx)
     ]
@@ -106,45 +164,36 @@
         for source, target in ((wo, zo), (wu, zu), (wd, zd))
         for device in over_dp
     ]
-    for copy in along + across[0]:
+    spread = Spread(dp, ctx, [None], [w_full], mover)
+    for copy in own[:1] + along:
         copy.start()
     moves[0].wait()
     moves[1].start()
     x[...] = wide[...].astype(BF)
-    for copy in rows + own + others:
+    for copy in rows + own[1:]:
+        copy.start()
+    for copy in along:
+        copy.wait_recv()
+    own[0].wait()
+    spread.begin()
+    for copy in others:
         copy.start()
     rest[...] = (wide[...] - x[...].astype(F32)).astype(BF)
     moves[2].start()
     moves[1].wait()
     up[...] = wide_up[...].astype(BF)
     moves[3].start()
-    for k in range(1, dp):
-        along[k - 1].wait_recv()
-        piece = w_full.at[(d - k + dp) % dp, c]
-        across.append([mover.remote(piece, piece, device) for device in over_groups])
-        for copy in across[-1]:
-            copy.start()
-    own[0].wait()
-    mine = w_full.at[:, c]
-    over = [mover.remote(mine, mine, sibling)]
-    over[0].start()
-    for k in range(1, groups):
-        for batch in across:
-            batch[k - 1].wait_recv()
-        block = w_full.at[:, (g - k + groups) % groups * 2 + m]
-        over.append(mover.remote(block, block, sibling))
-        over[-1].start()
-    for copy in over + rows + others + moves[2:]:
+    for level in range(1, spread.levels + 1):
+        spread.forward(0, level)
+    for copy in rows + others + moves[2:] + own[1:]:
         copy.wait()
-    for copy in along + [copy for batch in across for copy in batch]:
+    spread.finish()
+    for copy in along:
         copy.wait_send()
-    for copy in own[1:]:
-        copy.wait()
 
 
 def gather_first(tokens, cotangent, w, wo, wu, wd, dp, ctx):
-    groups = ctx // 2
-    remotes = (dp - 1) + dp * (groups - 1) + (ctx - 1) + 3 * (dp - 1) + groups
+    remotes = (dp - 1) + Spread.count(ctx, 1) + (ctx - 1) + 3 * (dp - 1)
     any_space = pl.BlockSpec(memory_space=pl.ANY)
     return pl.pallas_call(
         functools.partial(gather_kernel, dp, ctx),
@@ -166,44 +215,6 @@
         ),
         name="gather_first",
     )(tokens, cotangent, w, wo, wu, wd)
-
-
-class Spread:
-    def __init__(self, dp, ctx, sources, targets, mover):
-        d, c, g, m, over_dp, over_groups, sibling = place(dp, ctx)
-        groups = ctx // 2
-        self.devices = over_groups + [sibling]
-        self.own = [mover.local(s, t.at[:, c]) for s, t in zip(sources, targets)]
-        self.direct = [mover.remote(s, t.at[:, c], sibling) for s, t in zip(sources, targets)]
-        self.across = [
-            [mover.remote(s, t.at[:, c], device) for device in over_groups]
-            for s, t in zip(sources, targets)
-        ]
-        self.onward = []
-        for t in targets:
-            blocks = [t.at[:, (g - k + groups) % groups * 2 + m] for k in range(1, groups)]
-            self.onward.append([mover.remote(block, block, sibling) for block in blocks])
-
-    @staticmethod
-    def count(groups, arrays):
-        return arrays * (1 + 2 * (groups - 1))
-
-    def begin(self):
-        greet(self.devices)
-        for copy in self.own + [copy for batch in self.across for copy in batch] + self.direct:
-            copy.start()
-
-    def forward(self, index):
-        for came, copy in zip(self.across[index], self.onward[index]):
-            came.wait_recv()
-            copy.start()
-
-    def finish(self):
-        for copy in self.own + self.direct + [copy for batch in self.onward for copy in batch]:
-            copy.wait()
-        for batch in self.across:
-            for copy in batch:
-                copy.wait_send()
 
 
 class Scatter:
@@ -549,6 +560,7 @@
 
     @pl.when(step == 0)
     def _():
+        greet(spread.devices)
         spread.begin()
         project(pair)
 
@@ -585,13 +597,14 @@
     mb_ref[...] = mixed.astype(BF)
     lse_ref[0] = jnp.where(lane == 0, lses[0], lses[1]).T[:8]
 
-    for index, at in enumerate(last):
-
-        @pl.when(step == at)
-        def _(index=index):
-            spread.forward(index)
-
-    @pl.when(step == last[-1])
+    for index, ats in enumerate(last):
+        for level in range(1, spread.levels + 1):
+
+            @pl.when(step == ats[0] + (ats[1] - ats[0]) * (level - 1) // (spread.levels - 1))
+            def _(index=index, level=level):
+                spread.forward(index, level)
+
+    @pl.when(step == pairs * steps - 1)
     def _():
         spread.finish()
         for number in range(pairs):
@@ -607,7 +620,7 @@
     blk = pl.BlockSpec((bq, 128), lambda p, j: (j, p))
     any_space = pl.BlockSpec(memory_space=pl.ANY)
     vmem = pl.BlockSpec(memory_space=pltpu.VMEM)
-    remotes = Spread.count(ctx // 2, 3)
+    remotes = Spread.count(ctx, 3)
     return pl.pallas_call(
         functools.partial(forward_kernel, dp, ctx, bq),
         grid=(pairs, rows // bq),
@@ -641,7 +654,7 @@
 
 def forward_steps(pairs, steps):
     count = pairs * steps
-    return (count * 5 // 24, count * 15 // 24, count - 1)
+    return [(count * a // 24, count * b // 24) for a, b in ((11, 18), (12, 19), (13, 20))]
 
 
 def backward_steps(pairs, steps):
@@ -1074,7 +1087,7 @@
 
 
 def write_out(small, sums, out, tokens, own, held_up, dp, ctx):
-    block = pl.BlockSpec((1,) + out.shape[1:], lambda i: (i, 0, 0))
+    block = pl.BlockSpec((2,) + out.shape[1:], lambda i: (i, 0, 0))
     S = jax.ShapeDtypeStruct
 
     def whole(shape):
@@ -1084,7 +1097,7 @@
     vectors = (8, out.shape[2] // (dp * ctx))
     return pl.pallas_call(
         functools.partial(write_kernel, dp, ctx),
-        grid=(ctx,),
+        grid=(ctx // 2,),
         in_specs=[whole(small.shape), whole(sums.shape), block, block]
         + [whole(shape) for shape in shapes],
         out_specs=[block, block]

time: 360 us -> 352 us (0.978)
  Pallas kernels: 347 us -> 339 us
    pallas_call x1, Pallas kernels: 67 us -> 62.4 us  [attention_forward(): pl.pallas_call(functools.partial(forward_kernel, dp, ctx, bq), grid=(pair...]
    pallas_call x1, Pallas kernels: 47.7 us -> 43.9 us  [gather_first(): pl.pallas_call(functools.partial(gather_kernel, dp, ctx), in_specs=[any_s...]
where the time goes in v1:
time: 352 us; the launch traced here: 347 us
  Pallas kernels  339 us (96%)
  other arithmetic  3.54 us (1%)
    pallas_call x1, Pallas kernels, attention_backward(): pl.pallas_call(functools.partial(backward_kernel, dp, ctx, ck), grid=(pai...  93.2 us
    pallas_call x1, Pallas kernels, middle(): pl.pallas_call(functools.partial(middle_kernel, dp, ctx), grid=(ctx // 2...  79.1 us
    pallas_call x1, Pallas kernels, attention_forward(): pl.pallas_call(functools.partial(forward_kernel, dp, ctx, bq), grid=(pair...  62.4 us
    pallas_call x1, Pallas kernels, finish_gradients(): pl.pallas_call(functools.partial(finish_kernel, dp, ctx), in_specs=[vmem]...  55 us
    pallas_call x1, Pallas kernels, gather_first(): pl.pallas_call(functools.partial(gather_kernel, dp, ctx), in_specs=[any_s...  43.9 us

profile of v1, /device:TPU:1, one launch (start us, length us, event | category | flops | bytes accessed | tf_op | source)
XLA Modules:
  0.0 347.1 jit_solution(7447059557352450298)
XLA Ops:
  0.6 0.7 reshape.75
  1.4 0.8 copy.24
  2.2 0.1 fusion.2
  2.2 1.5 pad_maximum_fusion.refs_2_
  3.7 43.9 %gather_first.1 = (bf16[8,128,768]{2,1,0:T(8,128)(2,1)}, bf16[8,128,768]{2,1,0:T(8,128)(2,1)}, bf16[8,128,768]{2,1,0:T(8,128)(2,1)}, bf16[4,8,24,2432]{3,2,1,0:T...) custom-call(f32[8,128,768]{2,1,0:T(8,128)} %bitcast.19, ...), custom_call_target="tpu_custom_call" | custom-call | tf_op jit(solution)/shard_map/gather_first/pallas_call | solution.py:198
  47.6 1.0 slice_convert_fusion
  48.7 0.9 reshape.86.refs_5_
  49.5 1.0 convert_bitcast_fusion
  50.5 0.7 copy.25.refs_2_.refs_4_
  51.2 62.4 %attend.1 = (bf16[1024,768]{1,0:T(8,128)(2,1)}, f32[1024,768]{1,0:T(8,128)}, f32[6,8,1024]{2,1,0:T(8,128)}, bf16[6,3,1024,128]{3,2,1,0:T(8,128)(2,1)}, bf16[6,2,...) custom-call(bf16[1024,768]{1,0:T(8,128)(2,1)} %bitcast.21, ...), custom_call_target="tpu_custom_call" | custom-call | flops 12884901888 | bytes 11010048 | tf_op jit(solution)/shard_map/attend/pallas_call | solution.py:624
  113.7 79.1 %middle.1 = (bf16[1024,768]{1,0:T(8,128)(2,1)}, f32[1024,768]{1,0:T(8,128)}, bf16[8,128,768]{2,1,0:T(8,128)(2,1)}, bf16[768,768]{1,0:T(8,128)(2,1)}, bf16[768,30...) custom-call(bf16[1024,768]{1,0:T(8,128)(2,1)} %get-tuple-element.61.refs_0_, ...), custom_call_target="tpu_custom_call" | custom-call | flops 32614907904 | bytes 52428800 | tf_op jit(solution)/shard_map/middle/pallas_call | solution.py:1023
  192.7 93.2 %attend_back.1 = (bf16[1024,768]{1,0:T(8,128)(2,1)}, bf16[1024,768]{1,0:T(8,128)(2,1)}, bf16[1024,768]{1,0:T(8,128)(2,1)}, f32[24,768]{1,0:T(8,128)}, f32[96,768...) custom-call(bf16[6,3,1024,128]{3,2,1,0:T(8,128)(2,1)} %get-tuple-element.59.refs_0_.refs_1_.refs_2_, ...), custom_call_target="tpu_custom_call" | custom-call | flops 32212254720 | bytes 20447232 | tf_op jit(solution)/shard_map/attend_back/pallas_call | solution.py:818
  285.9 55.0 %finish_gradients.1 = (f32[24,768]{1,0:T(8,128)}, f32[24,768]{1,0:T(8,128)}, f32[24,768]{1,0:T(8,128)}, f32[8,768]{1,0:T(8,128)}, bf16[8,128,768]{2,1,0:T(8,128)(2,1)}) custom-call(bf16[1024,768]{1,0:T(8,128)(2,1)} %bitcast.23, bf16[1024,768]{1,0:T(8,128)(2,1)} %get-tuple-element.75.refs_1_, bf16[1024,768]{1,0:T(8,128)(2,1)} %get-tuple-element.76.refs_2_, ...), custom_call_target="tpu_custom_call" | custom-call | tf_op jit(solution)/shard_map/finish_gradients/pallas_call | solution.py:483
  340.9 5.7 %write_out.1 = (f32[8,128,768]{2,1,0:T(8,128)}, f32[8,128,768]{2,1,0:T(8,128)}, f32[24,768]{1,0:T(8,128)}, f32[24,768]{1,0:T(8,128)}, f32[24,768]{1,0:T(8,128)},...) custom-call(f32[16,768]{1,0:T(8,128)} %get-tuple-element.74.small_ref, ...), custom_call_target="tpu_custom_call" | custom-call | tf_op jit(solution)/shard_map/write_out/pallas_call | solution.py:1098

commit v2 on v1

--- a/solution.py
+++ b/solution.py
@@ -408,15 +408,23 @@
 
 
 def finish_kernel(dp, ctx, *refs):
-    (xb, dq, dk, dv, w, grad_sum), refs = refs[:6], refs[6:]
+    loaded, refs = refs[:6], refs[6:]
     outs, small_out, x_out, refs = refs[:3], refs[3], refs[4], refs[5:]
     grads, result, small, refs = refs[:3], refs[3], refs[4], refs[5:]
-    buffers, small_buffers, (local_sem, send_sem, recv_sem) = refs[:15], refs[15:21], refs[21:]
+    (xb, dq, dk, dv, w, grad_sum), refs = refs[:6], refs[6:]
+    buffers, small_buffers, refs = refs[:15], refs[15:21], refs[21:]
+    local_sem, send_sem, recv_sem, load_sem = refs
+    loads = [
+        pltpu.make_async_copy(source, target, load_sem.at[i])
+        for i, (source, target) in enumerate(zip(loaded, (xb, dq, dk, dv, w, grad_sum)))
+    ]
+    for copy in loads:
+        copy.start()
     d, c = lax.axis_index("dp"), lax.axis_index("ctx")
     groups = ctx // 2
     g = c // 2
     half, width = result.shape[1:]
-    held = grads[0].shape[3]
+    held, late = grads[0].shape[3:]
     mover = Mover(local_sem, send_sem, recv_sem)
     scatter = Scatter(
         dp,
@@ -432,14 +440,12 @@
     give = Exchange(ctx, mover, result, x_out)
     greet([((d + k) % dp, c) for k in range(1, dp)] + [(d, (c + k) % ctx) for k in range(1, ctx)])
     small[...] = jnp.zeros_like(small)
-    small[0:1, :] = columns(dq[...].astype(F32))
-    small[1:2, :] = columns(dv[...].astype(F32))
-    scatter.begin_small()
-
+    loads[0].wait()
     across = xb[...].T
 
     def weight_gradient(index, rows_grad):
-        total = dg(across, rows_grad[...], NN)
+        loads[1 + index].wait()
+        total = dg(across, rows_grad[:, width - late :], NN)
         for block in range(dp * ctx):
             at = (block // ctx, block % ctx // 2, block % 2)
             grads[index][at] = total[block * held : (block + 1) * held].astype(BF)
@@ -455,12 +461,20 @@
         give.start(t)
 
     tiles = list(range(groups - 1, -1, -1))
-    for index, rows_grad in enumerate((dq, dk, dv)):
-        weight_gradient(index, rows_grad)
-        row_tile(tiles.pop(0))
-        if index == 0:
-            scatter.first_small()
-        scatter.first(index)
+    weight_gradient(0, dq)
+    weight_gradient(1, dk)
+    scatter.first(0)
+    weight_gradient(2, dv)
+    scatter.first(1)
+    for copy in loads[4:]:
+        copy.wait()
+    row_tile(tiles.pop(0))
+    scatter.first(2)
+    small[0:1, :] = columns(dq[...].astype(F32))
+    small[1:2, :] = columns(dv[...].astype(F32))
+    scatter.begin_small()
+    row_tile(tiles.pop(0))
+    scatter.first_small()
     for t in tiles:
         row_tile(t)
     scatter.middle_small()
@@ -477,21 +491,24 @@
     remotes = Scatter.count(dp, ctx, 3) + Exchange.count(ctx)
     S = jax.ShapeDtypeStruct
     vmem = pl.BlockSpec(memory_space=pltpu.VMEM)
-    source = S((dp, ctx // 2, 2, width // (dp * ctx), width), BF)
+    late = width - width // 256 * 128
+    source = S((dp, ctx // 2, 2, width // (dp * ctx), late), BF)
     small = S((8, width), F32)
     moved = (ctx, rows // ctx, width)
     return pl.pallas_call(
         functools.partial(finish_kernel, dp, ctx),
-        in_specs=[vmem] * 6,
+        in_specs=[pl.BlockSpec(memory_space=pl.ANY)] * 6,
         out_specs=[vmem] * 4 + [pl.BlockSpec(memory_space=pl.ANY)],
         out_shape=[S(source.shape[3:], F32)] * 3 + [small, S(moved, BF)],
         scratch_shapes=[pltpu.VMEM(source.shape, BF)] * 3
         + [pltpu.VMEM(moved, BF), pltpu.VMEM(small.shape, F32)]
+        + [pltpu.VMEM(array.shape, array.dtype) for array in (xb, dq, dk, dv, w, grad_sum)]
         + Scatter.scratch(dp, ctx, [source] * 3, small)
         + [
             pltpu.SemaphoreType.DMA((4,)),
             pltpu.SemaphoreType.DMA((remotes,)),
             pltpu.SemaphoreType.DMA((remotes,)),
+            pltpu.SemaphoreType.DMA((6,)),
         ],
         compiler_params=pltpu.CompilerParams(
             collective_id=3, has_side_effects=True, vmem_limit_bytes=VMEM_BYTES
@@ -659,8 +676,8 @@
 
 def backward_steps(pairs, steps):
     count = pairs * steps
-    first = [count * at // 12 for at in (0, 0, 1)]
-    middle = [count * at // 12 for at in (5, 4, 8)]
+    first = [count * at // 12 for at in (0, 0, 1, 7)]
+    middle = [count * at // 12 for at in (5, 4, 8, 10)]
     return first, middle
 
 
@@ -672,18 +689,18 @@
     q_ref, ko_ref, vo_ref, ks_ref, vs_ref = (
         ref.at[0, 0] for ref in (q_ref, ko_ref, vo_ref, ks_ref, vs_ref)
     )
-    sources, small, refs = refs[:3], refs[3], refs[4:]
+    sources, small, x_ref, refs = refs[:3], refs[3], refs[4], refs[5:]
     (dq_ref, dk_ref, dv_ref), refs = refs[:3], refs[3:]
-    summed, small_out, refs = refs[:3], refs[3], refs[4:]
-    (keys, dk, dv, held, going, coming), refs = refs[:6], refs[6:]
-    buffers, small_buffers, refs = refs[:15], refs[15:21], refs[21:]
+    summed, small_out, refs = refs[:4], refs[4], refs[5:]
+    (keys, dk, dv, held, going, coming, across, dq_held, early), refs = refs[:9], refs[9:]
+    buffers, small_buffers, refs = refs[:20], refs[20:26], refs[26:]
     local_sem, send_sem, recv_sem, pair_send, pair_recv = refs
     scatter = Scatter(
         dp,
         ctx,
-        sources,
+        [*sources, early],
         summed,
-        [buffers[i * 5 : i * 5 + 5] for i in range(3)],
+        [buffers[i * 5 : i * 5 + 5] for i in range(4)],
         small,
         small_out,
         small_buffers,
@@ -711,10 +728,13 @@
 
     def settle(number):
         lanes = pl.ds(pl.multiple_of(number * 128, 128), 128)
+        totals = []
         for i, (copy, out) in enumerate(zip(to_sibling(number), (dk_ref, dv_ref))):
             copy.wait_recv()
             total = held[number % 2, i] + coming[number, i].astype(F32)
-            out[:, lanes] = total.astype(BF)
+            totals.append(total.astype(BF))
+            out[:, lanes] = totals[-1]
+        return totals
 
     @pl.when(step == 0)
     def _():
@@ -723,8 +743,26 @@
         scatter.begin_small()
         scatter.begin(0)
         scatter.begin(2)
-
-    @pl.when((j == 0) & (pair > 0))
+        across[...] = x_ref[...].T
+
+    early_pairs = early.shape[4] // 384
+
+    @pl.when((j == 0) & (pair > 0) & (pair <= early_pairs))
+    def _():
+        rows_grad = jnp.concatenate([dq_held[...], *settle(pair - 1)], axis=1)
+        total = dg(across[...], rows_grad, NN)
+        lanes = pl.ds(pl.multiple_of((pair - 1) * 384, 128), 384)
+        owned = early.shape[3]
+        for block in range(dp * ctx):
+            at = (block // ctx, block % ctx // 2, block % 2)
+            part = total[block * owned : (block + 1) * owned]
+            early[(*at, slice(None), lanes)] = part.astype(BF)
+
+    @pl.when((j == 0) & (pair == early_pairs))
+    def _():
+        scatter.begin(3)
+
+    @pl.when((j == 0) & (pair > early_pairs))
     def _():
         settle(pair - 1)
 
@@ -763,7 +801,9 @@
             dv[rows, :] += dg(p.astype(BF), dom, NN)
             dk[rows, :] += dg(ds, qz, NN)
             dq = dq + dg(ds, k, TN)
-    dq_ref[...] = (dq * 0.125).astype(BF)
+    low_dq = (dq * 0.125).astype(BF)
+    dq_ref[...] = low_dq
+    dq_held[pl.ds(pl.multiple_of(j * bq, bq), bq), :] = low_dq
 
     @pl.when(j == steps - 1)
     def _():
@@ -783,7 +823,7 @@
     def _():
         scatter.middle_small()
 
-    for index in range(3):
+    for index in range(4):
 
         @pl.when(step == first[index])
         def _(index=index):
@@ -802,7 +842,9 @@
                 copy.wait_send()
 
 
-def attention_backward(own, sib, do, mix, lengths, lse, sources, small, dp, ctx, bq=512, ck=512):
+def attention_backward(
+    own, sib, do, mix, lengths, lse, sources, small, x, dp, ctx, bq=512, ck=512
+):
     rows, width = do.shape
     pairs = width // 128
     S = jax.ShapeDtypeStruct
@@ -811,9 +853,13 @@
         pl.BlockSpec((1, 1, rows, 128), lambda p, j, i=i: (p, i, 0, 0)) for i in (1, 2, 0, 1)
     ]
     any_space = pl.BlockSpec(memory_space=pl.ANY)
-    remotes = Scatter.count(dp, ctx, 3)
+    early = jax.ShapeDtypeStruct(
+        (dp, ctx // 2, 2, width // (dp * ctx), pairs // 2 * 384), BF
+    )
+    every = [*sources, early]
+    remotes = Scatter.count(dp, ctx, 4)
     whole = pl.BlockSpec(small.shape, lambda p, j: (0, 0))
-    sums = [s.shape[-2:] for s in sources]
+    sums = [s.shape[-2:] for s in every]
     all_rows = pl.BlockSpec((rows, width), lambda p, j: (0, 0))
     return pl.pallas_call(
         functools.partial(backward_kernel, dp, ctx, ck),
@@ -824,7 +870,7 @@
         + [pl.BlockSpec(memory_space=pltpu.SMEM)]
         + [pl.BlockSpec((1, 8, bq), lambda p, j: (p, 0, j))]
         + [any_space] * 3
-        + [whole],
+        + [whole, pl.BlockSpec(memory_space=pltpu.VMEM)],
         out_specs=[blk, all_rows, all_rows]
         + [pl.BlockSpec(shape, lambda p, j: (0, 0)) for shape in sums]
         + [whole],
@@ -838,10 +884,13 @@
             pltpu.VMEM((2, 2, rows, 128), F32),
             pltpu.VMEM((pairs, 2, rows, 128), BF),
             pltpu.VMEM((pairs, 2, rows, 128), BF),
+            pltpu.VMEM((width, rows), BF),
+            pltpu.VMEM((rows, 128), BF),
+            pltpu.VMEM(early.shape, BF),
         ]
-        + Scatter.scratch(dp, ctx, sources, small)
+        + Scatter.scratch(dp, ctx, every, small)
         + [
-            pltpu.SemaphoreType.DMA((3,)),
+            pltpu.SemaphoreType.DMA((4,)),
             pltpu.SemaphoreType.DMA((remotes,)),
             pltpu.SemaphoreType.DMA((remotes,)),
             pltpu.SemaphoreType.DMA((2 * pairs,)),
@@ -856,7 +905,7 @@
             transcendentals=4 * rows * rows * pairs,
         ),
         name="attend_back",
-    )(own, own, own, sib, sib, do, mix, lengths, lse, *sources, small)
+    )(own, own, own, sib, sib, do, mix, lengths, lse, *sources, small, x)
 
 
 def gelu_and_slope(x):
@@ -1066,14 +1115,21 @@
 
 
 def write_kernel(dp, ctx, small_ref, sums_ref, out_ref, tokens_ref, *refs):
-    sources, (out_to, tokens_to), refs = refs[:6], refs[6:8], refs[8:]
+    sources, early, (out_to, tokens_to), refs = refs[:6], refs[6], refs[7:9], refs[9:]
     targets, (vectors_to, bias_to) = refs[:6], refs[6:]
     out_to[...] = out_ref[...].astype(F32)
     tokens_to[...] = tokens_ref[...].astype(F32)
 
     @pl.when(pl.program_id(0) == 0)
     def _():
-        for source, target in zip(sources, targets):
+        for i in range(3):
+            late = sources[i].shape[1]
+            first = targets[i].shape[1] - late
+            targets[i][:, first:] = sources[i][...]
+            for lane in range(0, first, 128):
+                at = lane * 3 + i * 128
+                targets[i][:, lane : lane + 128] = early[:, at : at + 128]
+        for source, target in zip(sources[3:], targets[3:]):
             target[...] = source[...]
         device = lax.axis_index("dp") * ctx + lax.axis_index("ctx")
         width = small_ref.shape[1]
@@ -1086,20 +1142,21 @@
         bias_to[...] = pltpu.roll(row, (width - first % width) % width, 1)[0:1, :held_up]
 
 
-def write_out(small, sums, out, tokens, own, held_up, dp, ctx):
+def write_out(small, sums, out, tokens, own, early, held_up, dp, ctx):
     block = pl.BlockSpec((2,) + out.shape[1:], lambda i: (i, 0, 0))
     S = jax.ShapeDtypeStruct
 
     def whole(shape):
         return pl.BlockSpec(shape, lambda i: (0, 0))
 
-    shapes = [array.shape for array in own]
+    given = [array.shape for array in (*own, early)]
+    shapes = [(own[0].shape[0], out.shape[2])] * 3 + [array.shape for array in own[3:]]
     vectors = (8, out.shape[2] // (dp * ctx))
     return pl.pallas_call(
         functools.partial(write_kernel, dp, ctx),
         grid=(ctx // 2,),
         in_specs=[whole(small.shape), whole(sums.shape), block, block]
-        + [whole(shape) for shape in shapes],
+        + [whole(shape) for shape in given],
         out_specs=[block, block]
         + [whole(shape) for shape in shapes]
         + [whole(vectors), whole((1, held_up))],
@@ -1108,7 +1165,7 @@
         + [S(vectors, F32), S((1, held_up), F32)],
         compiler_params=pltpu.CompilerParams(vmem_limit_bytes=VMEM_BYTES),
         name="write_out",
-    )(small, sums, out, tokens, *own)
+    )(small, sums, out, tokens, *own, early)
 
 
 def on_device(
@@ -1161,7 +1218,7 @@
         dp,
         ctx,
     )
-    dq, dk, dv, own_attn, own_down, own_up, small = attention_backward(
+    dq, dk, dv, own_attn, own_down, own_up, own_early, small = attention_backward(
         own,
         sib,
         d_mixed,
@@ -1170,6 +1227,7 @@
         lse,
         [by_owner(d_attn), part_down, by_owner(d_up)],
         small,
+        low_in,
         dp,
         ctx,
     )
@@ -1182,6 +1240,7 @@
         result,
         grad_tokens,
         [own_query, own_key, own_value, own_attn, own_up, own_down],
+        own_early,
         b_up.shape[0],
         dp,
         ctx,

time: 352 us -> 341 us (0.969); the launches traced: 347 us -> 341 us
  Pallas kernels: 339 us -> 333 us
    pallas_call x1, Pallas kernels: 55 us -> 44.5 us  [finish_gradients(): pl.pallas_call(functools.partial(finish_kernel, dp, ctx), in_specs=[pl.Bl...]
    pallas_call x1, Pallas kernels: 93.2 us -> 97.6 us  [attention_backward(): pl.pallas_call(functools.partial(backward_kernel, dp, ctx, ck), grid=(pai...]
where the time goes in v2:
time: 341 us
  Pallas kernels  333 us (98%)
  other arithmetic  3.54 us (1%)
    pallas_call x1, Pallas kernels, attention_backward(): pl.pallas_call(functools.partial(backward_kernel, dp, ctx, ck), grid=(pai...  97.6 us
    pallas_call x1, Pallas kernels, middle(): pl.pallas_call(functools.partial(middle_kernel, dp, ctx), grid=(ctx // 2...  79 us
    pallas_call x1, Pallas kernels, attention_forward(): pl.pallas_call(functools.partial(forward_kernel, dp, ctx, bq), grid=(pair...  62.4 us
    pallas_call x1, Pallas kernels, finish_gradients(): pl.pallas_call(functools.partial(finish_kernel, dp, ctx), in_specs=[pl.Bl...  44.5 us
    pallas_call x1, Pallas kernels, gather_first(): pl.pallas_call(functools.partial(gather_kernel, dp, ctx), in_specs=[any_s...  43.9 us

profile of v2, /device:TPU:1, one launch (start us, length us, event | category | flops | bytes accessed | tf_op | source)
XLA Modules:
  0.0 341.0 jit_solution(16129806225190319913)
XLA Ops:
  0.6 0.7 reshape.75
  1.4 0.8 copy.24
  2.2 0.1 fusion.2
  2.2 1.5 pad_maximum_fusion.refs_2_
  3.7 43.9 %gather_first.1 = (bf16[8,128,768]{2,1,0:T(8,128)(2,1)}, bf16[8,128,768]{2,1,0:T(8,128)(2,1)}, bf16[8,128,768]{2,1,0:T(8,128)(2,1)}, bf16[4,8,24,2432]{3,2,1,0:T...) custom-call(f32[8,128,768]{2,1,0:T(8,128)} %bitcast.19, ...), custom_call_target="tpu_custom_call" | custom-call | tf_op jit(solution)/shard_map/gather_first/pallas_call | solution.py:198
  47.6 1.0 slice_convert_fusion
  48.7 0.9 reshape.86.refs_5_
  49.5 1.0 convert_bitcast_fusion
  50.5 0.7 copy.25.refs_2_.refs_4_
  51.2 62.4 %attend.1 = (bf16[1024,768]{1,0:T(8,128)(2,1)}, f32[1024,768]{1,0:T(8,128)}, f32[6,8,1024]{2,1,0:T(8,128)}, bf16[6,3,1024,128]{3,2,1,0:T(8,128)(2,1)}, bf16[6,2,...) custom-call(bf16[1024,768]{1,0:T(8,128)(2,1)} %bitcast.21, ...), custom_call_target="tpu_custom_call" | custom-call | flops 12884901888 | bytes 11010048 | tf_op jit(solution)/shard_map/attend/pallas_call | solution.py:641
  113.7 79.0 %middle.1 = (bf16[1024,768]{1,0:T(8,128)(2,1)}, f32[1024,768]{1,0:T(8,128)}, bf16[8,128,768]{2,1,0:T(8,128)(2,1)}, bf16[768,768]{1,0:T(8,128)(2,1)}, bf16[768,30...) custom-call(bf16[1024,768]{1,0:T(8,128)(2,1)} %get-tuple-element.62.refs_0_, ...), custom_call_target="tpu_custom_call" | custom-call | flops 32614907904 | bytes 52428800 | tf_op jit(solution)/shard_map/middle/pallas_call | solution.py:1072
  192.7 97.6 %attend_back.1 = (bf16[1024,768]{1,0:T(8,128)(2,1)}, bf16[1024,768]{1,0:T(8,128)(2,1)}, bf16[1024,768]{1,0:T(8,128)(2,1)}, f32[24,768]{1,0:T(8,128)}, f32[96,768...) custom-call(bf16[6,3,1024,128]{3,2,1,0:T(8,128)(2,1)} %get-tuple-element.60.refs_0_.refs_1_.refs_2_, ...), custom_call_target="tpu_custom_call" | custom-call | flops 32212254720 | bytes 20447232 | tf_op jit(solution)/shard_map/attend_back/pallas_call | solution.py:864
  290.3 44.5 %finish_gradients.1 = (f32[24,384]{1,0:T(8,128)}, f32[24,384]{1,0:T(8,128)}, f32[24,384]{1,0:T(8,128)}, f32[8,768]{1,0:T(8,128)}, bf16[8,128,768]{2,1,0:T(8,128)(2,1)}) custom-call(bf16[1024,768]{1,0:T(8,128)(2,1)} %bitcast.24, bf16[1024,768]{1,0:T(8,128)(2,1)} %get-tuple-element.76.refs_1_, bf16[1024,768]{1,0:T(8,128)(2,1)} %get-tuple-element.77.refs_2_, ...), custom_call_target="tpu_custom_call" | custom-call | tf_op jit(solution)/shard_map/finish_gradients/pallas_call | solution.py:498
  334.7 5.8 %write_out.1 = (f32[8,128,768]{2,1,0:T(8,128)}, f32[8,128,768]{2,1,0:T(8,128)}, f32[24,768]{1,0:T(8,128)}, f32[24,768]{1,0:T(8,128)}, f32[24,768]{1,0:T(8,128)},...) custom-call(f32[16,768]{1,0:T(8,128)} %get-tuple-element.75.small_ref, ...), custom_call_target="tpu_custom_call" | custom-call | tf_op jit(solution)/shard_map/write_out/pallas_call | solution.py:1155

commit v3 on v2

--- a/solution.py
+++ b/solution.py
@@ -843,7 +843,7 @@
 
 
 def attention_backward(
-    own, sib, do, mix, lengths, lse, sources, small, x, dp, ctx, bq=512, ck=512
+    own, sib, do, mix, lengths, lse, sources, small, x, dp, ctx, bq=1024, ck=256
 ):
     rows, width = do.shape
     pairs = width // 128
@@ -909,7 +909,7 @@
 
 
 def gelu_and_slope(x):
-    t = 1.0 / (1.0 + 0.2316419 * jnp.abs(x))
+    t = pl.reciprocal(1.0 + 0.2316419 * jnp.abs(x))
     bell = 0.3989422804 * jnp.exp(-0.5 * x * x)
     poly = 1.330274429 * t - 1.821255978
     poly = poly * t + 1.781477937
@@ -1143,7 +1143,7 @@
 
 
 def write_out(small, sums, out, tokens, own, early, held_up, dp, ctx):
-    block = pl.BlockSpec((2,) + out.shape[1:], lambda i: (i, 0, 0))
+    block = pl.BlockSpec((ctx // 2,) + out.shape[1:], lambda i: (i, 0, 0))
     S = jax.ShapeDtypeStruct
 
     def whole(shape):
@@ -1154,7 +1154,7 @@
     vectors = (8, out.shape[2] // (dp * ctx))
     return pl.pallas_call(
         functools.partial(write_kernel, dp, ctx),
-        grid=(ctx // 2,),
+        grid=(2,),
         in_specs=[whole(small.shape), whole(sums.shape), block, block]
         + [whole(shape) for shape in given],
         out_specs=[block, block]

time: 341 us -> 338 us (level)
  Pallas kernels: 333 us -> 329 us
where the time goes in v3:
time: 338 us; the launch traced here: 336 us
  Pallas kernels  329 us (97%)
  other arithmetic  3.54 us (1%)
    pallas_call x1, Pallas kernels, attention_backward(): pl.pallas_call(functools.partial(backward_kernel, dp, ctx, ck), grid=(pai...  94.8 us
    pallas_call x1, Pallas kernels, middle(): pl.pallas_call(functools.partial(middle_kernel, dp, ctx), grid=(ctx // 2...  76.5 us
    pallas_call x1, Pallas kernels, attention_forward(): pl.pallas_call(functools.partial(forward_kernel, dp, ctx, bq), grid=(pair...  62.4 us
    pallas_call x1, Pallas kernels, finish_gradients(): pl.pallas_call(functools.partial(finish_kernel, dp, ctx), in_specs=[pl.Bl...  46.1 us
    pallas_call x1, Pallas kernels, gather_first(): pl.pallas_call(functools.partial(gather_kernel, dp, ctx), in_specs=[any_s...  43.9 us

profile of v3, /device:TPU:1, one launch (start us, length us, event | category | flops | bytes accessed | tf_op | source)
XLA Modules:
  0.0 336.4 jit_solution(5325417670428658339)
XLA Ops:
  0.6 0.7 reshape.75
  1.4 0.8 copy.24
  2.2 0.1 fusion.2
  2.2 1.5 pad_maximum_fusion.refs_2_
  3.7 43.9 %gather_first.1 = (bf16[8,128,768]{2,1,0:T(8,128)(2,1)}, bf16[8,128,768]{2,1,0:T(8,128)(2,1)}, bf16[8,128,768]{2,1,0:T(8,128)(2,1)}, bf16[4,8,24,2432]{3,2,1,0:T...) custom-call(f32[8,128,768]{2,1,0:T(8,128)} %bitcast.19, ...), custom_call_target="tpu_custom_call" | custom-call | tf_op jit(solution)/shard_map/gather_first/pallas_call | solution.py:198
  47.6 1.0 slice_convert_fusion
  48.7 0.9 reshape.86.refs_5_
  49.5 1.0 convert_bitcast_fusion
  50.5 0.7 copy.25.refs_2_.refs_4_
  51.2 62.4 %attend.1 = (bf16[1024,768]{1,0:T(8,128)(2,1)}, f32[1024,768]{1,0:T(8,128)}, f32[6,8,1024]{2,1,0:T(8,128)}, bf16[6,3,1024,128]{3,2,1,0:T(8,128)(2,1)}, bf16[6,2,...) custom-call(bf16[1024,768]{1,0:T(8,128)(2,1)} %bitcast.21, ...), custom_call_target="tpu_custom_call" | custom-call | flops 12884901888 | bytes 11010048 | tf_op jit(solution)/shard_map/attend/pallas_call | solution.py:641
  113.7 76.5 %middle.1 = (bf16[1024,768]{1,0:T(8,128)(2,1)}, f32[1024,768]{1,0:T(8,128)}, bf16[8,128,768]{2,1,0:T(8,128)(2,1)}, bf16[768,768]{1,0:T(8,128)(2,1)}, bf16[768,30...) custom-call(bf16[1024,768]{1,0:T(8,128)(2,1)} %get-tuple-element.62.refs_0_, ...), custom_call_target="tpu_custom_call" | custom-call | flops 32614907904 | bytes 52428800 | tf_op jit(solution)/shard_map/middle/pallas_call | solution.py:1072
  190.2 94.8 %attend_back.1 = (bf16[1024,768]{1,0:T(8,128)(2,1)}, bf16[1024,768]{1,0:T(8,128)(2,1)}, bf16[1024,768]{1,0:T(8,128)(2,1)}, f32[24,768]{1,0:T(8,128)}, f32[96,768...) custom-call(bf16[6,3,1024,128]{3,2,1,0:T(8,128)(2,1)} %get-tuple-element.60.refs_0_.refs_1_.refs_2_, ...), custom_call_target="tpu_custom_call" | custom-call | flops 32212254720 | bytes 20447232 | tf_op jit(solution)/shard_map/attend_back/pallas_call | solution.py:864
  285.1 46.1 %finish_gradients.1 = (f32[24,384]{1,0:T(8,128)}, f32[24,384]{1,0:T(8,128)}, f32[24,384]{1,0:T(8,128)}, f32[8,768]{1,0:T(8,128)}, bf16[8,128,768]{2,1,0:T(8,128)(2,1)}) custom-call(bf16[1024,768]{1,0:T(8,128)(2,1)} %bitcast.24, bf16[1024,768]{1,0:T(8,128)(2,1)} %get-tuple-element.76.refs_1_, bf16[1024,768]{1,0:T(8,128)(2,1)} %get-tuple-element.77.refs_2_, ...), custom_call_target="tpu_custom_call" | custom-call | tf_op jit(solution)/shard_map/finish_gradients/pallas_call | solution.py:498
  331.2 5.0 %write_out.1 = (f32[8,128,768]{2,1,0:T(8,128)}, f32[8,128,768]{2,1,0:T(8,128)}, f32[24,768]{1,0:T(8,128)}, f32[24,768]{1,0:T(8,128)}, f32[24,768]{1,0:T(8,128)},...) custom-call(f32[16,768]{1,0:T(8,128)} %get-tuple-element.75.small_ref, ...), custom_call_target="tpu_custom_call" | custom-call | tf_op jit(solution)/shard_map/write_out/pallas_call | solution.py:1155
